TPU v7x, 32 devices: a whole 2x2x4 slice. The times are simulated.
32 devices in a mesh: edge: 8 (over y, x, core), feat: 4 (over z).
Axes of the slice: x: 2, y: 2, z: 4, core: 2. Of those that a mesh axis runs over, the one named last changes fastest.
Arguments:
- node_latents: bfloat16 [4, 4096, 256], P('feat', 'edge'), may hold values from -6 to 6
- edge_latents: bfloat16 [4, 32768, 256], P('feat', 'edge'), may hold values from -6 to 6
- senders: int32 [32768], P('edge'), may hold values from 0 to 4095, as said below
- receivers: int32 [32768], P('edge'), may hold values from 0 to 4095, as said below
- regions: int32 [32768], P('edge'), may hold values from 0 to 23
- forced: int32 [4096], P('edge'), may hold values 0 or 1
- params: float32 [1824, 256], P('feat'), may hold values from -1.5 to 1.5, as said below
- first_moment: float32 [1824, 256], P('feat'), may hold values from -0.34 to 0.34
- second_moment: float32 [1824, 256], P('feat'), may hold values from 0.004 to 0.22
- averaged: float32 [1824, 256], P('feat'), may hold values from -1.7 to 1.7
- step: int32 [1], replicated, may hold values from 1 to 20
- cotangent: float32 [4, 4096, 256], P('feat', 'edge'), may hold values from -6 to 6
Outputs:
- new_latents: float32 [4, 4096, 256], P('feat', 'edge')
- grad_latents: float32 [4, 4096, 256], P('feat', 'edge')
- grad_edges: bfloat16 [4, 32768, 256], P('feat', 'edge')
- new_first: float32 [1824, 256], P('feat')
- new_second: float32 [1824, 256], P('feat')
- new_params: float32 [1824, 256], P('feat')
- new_average: float32 [1824, 256], P('feat')
- grad_norm: float32 [1], replicated
- vector_grads: float32 [8, 256], replicated
Inputs may be any that keep to these rules, and one draw needn't show every extreme that they name: `senders`: nodes are numbered so that node block b is nodes b * 512 to (b + 1) * 512 - 1. Edge k lies in edge block e = k // 4096; its sender lies in node block e - 1, e or e + 1, taken cyclically over the 4096 nodes. `receivers`: the receiver of edge k lies in node block e - 1, e or e + 1 of its edge block e = k // 4096, taken cyclically. `params`: parameters scaled by fan-in; gains near one.
All inputs are finite; a program needn't handle non-finite values. No bound on the sum of `forced` on one device may be relied on, other than what follows from the above.
Results may differ from a plain program's by a relative error of at most 0.0039.
The roundings to bfloat16 on the way count: a program that leaves them out, or rounds other values in their place, can miss the bound.
Values may be sent and summed in bfloat16 or wider, within the bound.
No kernel may reach another device: no remote copies, remote signals or barrier semaphores. Data moves between devices by JAX's collectives and lax.ppermute only.
A program may use at most 128 MiB of HBM per device.

v0:
```python
import jax
import jax.numpy as jnp
from jax import lax
from jax.sharding import PartitionSpec as P

NORM_EPS = 1e-05
MAX_NORM = 512.0
RATE = 0.05
BETA_ONE = 0.9
BETA_TWO = 0.95
ADAM_EPS = 1e-08
WEIGHT_DECAY = 0.1
AVERAGE_DECAY = 0.999


def padded(cells, sides, width):
    for axis, dim in sides:
        count = lax.axis_size(axis)
        head = lax.slice_in_dim(cells, 0, width, axis=dim)
        tail = lax.slice_in_dim(cells, cells.shape[dim] - width, cells.shape[dim], axis=dim)
        cells = jnp.concatenate(
            [
                lax.ppermute(tail, axis, [(i, (i + 1) % count) for i in range(count)]),
                cells,
                lax.ppermute(head, axis, [((i + 1) % count, i) for i in range(count)]),
            ],
            axis=dim,
        )
    return cells


def passed_along(value, axis, steps):
    count = lax.axis_size(axis)
    pairs = [(source, (source + steps) % count) for source in range(count)]
    return lax.ppermute(value, axis, pairs)


def product(left, right):
    return jnp.dot(left, right, preferred_element_type=jnp.float32)


def outer_product(left, right):
    return lax.dot_general(
        left, right, (((0,), (0,)), ((), ())), preferred_element_type=jnp.float32
    )


def product_transposed(left, right):
    return lax.dot_general(
        left, right, (((1,), (1,)), ((), ())), preferred_element_type=jnp.float32
    )


def pick_rows(table, indices):
    return jnp.take(table, indices, axis=0)


def add_rows(values, indices, rows):
    return jax.ops.segment_sum(values, indices, num_segments=rows)


def normalized(values):
    center = values - jnp.mean(values, axis=-1, keepdims=True)
    spread = jnp.mean(center * center, axis=-1, keepdims=True)
    inverse = lax.rsqrt(spread + NORM_EPS)
    return (center * inverse, inverse)


def layer_norm(values, gain, shift):
    unit, inverse = normalized(values)
    return unit * gain + shift


def norm_backward(values, gain, upstream):
    unit, inverse = normalized(values)
    scaled = upstream * gain
    inner = (
        scaled
        - jnp.mean(scaled, axis=-1, keepdims=True)
        - unit * jnp.mean(scaled * unit, axis=-1, keepdims=True)
    )
    return (inverse * inner, jnp.sum(upstream * unit, axis=0), jnp.sum(upstream, axis=0))


def silu_slope(values):
    sigma = jax.nn.sigmoid(values)
    return sigma * (1.0 + values * (1.0 - sigma))


def neighbourhood(latents):
    return padded(latents, (("edge", 0),), latents.shape[0])


def on_device(
    node_latents,
    edge_latents,
    senders,
    receivers,
    regions,
    forced,
    params,
    first_moment,
    second_moment,
    averaged,
    step,
    cotangent,
):
    latents = node_latents[0]
    edges = edge_latents[0]
    upstream = cotangent[0]
    width = latents.shape[1]
    node_rows = latents.shape[0]
    total_nodes = node_rows * lax.axis_size("edge")
    lowest = (lax.axis_index("edge") - 1) * node_rows
    send_local = jnp.mod(senders - lowest, total_nodes)
    recv_local = jnp.mod(receivers - lowest, total_nodes)
    weights = lax.all_gather(params.astype(jnp.bfloat16), "feat", axis=0, tiled=True)
    first = weights[0 : 3 * width]
    second = weights[3 * width : 4 * width]
    node_first = weights[4 * width : 6 * width]
    node_second = weights[6 * width : 7 * width]
    vectors = weights[7 * width : 7 * width + 8].astype(jnp.float32)
    table = weights[7 * width + 8 :]
    region_onehot = jax.nn.one_hot(regions, table.shape[0], dtype=jnp.bfloat16)
    near_nodes = neighbourhood(latents)
    from_send = pick_rows(near_nodes, send_local)
    from_recv = pick_rows(near_nodes, recv_local)
    pre = product(from_send, first[0:width]) + product(from_recv, first[width : 2 * width])
    pre = (
        pre
        + product(edges, first[2 * width : 3 * width])
        + vectors[0]
        + product(region_onehot, table)
    )
    hidden = jax.nn.silu(pre).astype(jnp.bfloat16)
    inner = product(hidden, second) + vectors[1]
    from_send, from_recv, pre, hidden, inner = (from_send, from_recv, pre, hidden, inner)
    messages = layer_norm(inner, vectors[2], vectors[3])
    partial_value = add_rows(messages, recv_local, 3 * node_rows)
    from_below = passed_along(partial_value[2 * node_rows :], "edge", 1)
    from_above = passed_along(partial_value[0:node_rows], "edge", -1)
    aggregate = (partial_value[node_rows : 2 * node_rows] + from_below + from_above).astype(
        jnp.bfloat16
    )
    pre_node = (
        product(latents, node_first[0:width])
        + product(aggregate, node_first[width : 2 * width])
        + vectors[4]
    )
    hidden_node = jax.nn.silu(pre_node).astype(jnp.bfloat16)
    inner_node = product(hidden_node, node_second) + vectors[5]
    update = layer_norm(inner_node, vectors[6], vectors[7])
    keep = (1 - forced).astype(jnp.float32)[:, None]
    new_latents = latents.astype(jnp.float32) + keep * update
    d_update = upstream * keep
    d_inner_node, d_gain_node, d_shift_node = norm_backward(inner_node, vectors[6], d_update)
    d_inner_node = d_inner_node.astype(jnp.bfloat16)
    g_node_second = outer_product(hidden_node, d_inner_node)
    d_bias_node_second = jnp.sum(d_inner_node.astype(jnp.float32), axis=0)
    d_pre_node = (product_transposed(d_inner_node, node_second) * silu_slope(pre_node)).astype(
        jnp.bfloat16
    )
    g_node_first = jnp.concatenate(
        [outer_product(latents, d_pre_node), outer_product(aggregate, d_pre_node)], axis=0
    )
    d_bias_node_first = jnp.sum(d_pre_node.astype(jnp.float32), axis=0)
    d_from_nodes = product_transposed(d_pre_node, node_first[0:width])
    d_aggregate = product_transposed(d_pre_node, node_first[width : 2 * width]).astype(jnp.bfloat16)
    near_back = padded(d_aggregate, (("edge", 0),), node_rows)
    d_messages = pick_rows(near_back, recv_local).astype(jnp.float32)
    d_inner, d_gain_edge, d_shift_edge = norm_backward(inner, vectors[2], d_messages)
    d_inner = d_inner.astype(jnp.bfloat16)
    g_second = outer_product(hidden, d_inner)
    d_bias_second = jnp.sum(d_inner.astype(jnp.float32), axis=0)
    d_pre = (product_transposed(d_inner, second) * silu_slope(pre)).astype(jnp.bfloat16)
    g_first = jnp.concatenate(
        [
            outer_product(from_send, d_pre),
            outer_product(from_recv, d_pre),
            outer_product(edges, d_pre),
        ],
        axis=0,
    )
    d_bias_first = jnp.sum(d_pre.astype(jnp.float32), axis=0)
    g_table = outer_product(region_onehot, d_pre)
    d_send = product_transposed(d_pre, first[0:width])
    d_recv = product_transposed(d_pre, first[width : 2 * width])
    grad_edges = product_transposed(d_pre, first[2 * width : 3 * width]).astype(jnp.bfloat16)
    node_partial = add_rows(d_send, send_local, 3 * node_rows) + add_rows(
        d_recv, recv_local, 3 * node_rows
    )
    grads_below = passed_along(
        node_partial[2 * node_rows :].astype(jnp.bfloat16), "edge", 1
    ).astype(jnp.float32)
    grads_above = passed_along(node_partial[0:node_rows].astype(jnp.bfloat16), "edge", -1).astype(
        jnp.float32
    )
    d_nodes = node_partial[node_rows : 2 * node_rows] + grads_below + grads_above
    grad_latents = upstream + d_from_nodes + d_nodes
    vector_rows = jnp.stack(
        [
            d_bias_first,
            d_bias_second,
            d_gain_edge,
            d_shift_edge,
            d_bias_node_first,
            d_bias_node_second,
            d_gain_node,
            d_shift_node,
        ],
        axis=0,
    )
    local_grad = jnp.concatenate(
        [g_first, g_second, g_node_first, g_node_second, vector_rows, g_table], axis=0
    )
    share = params.shape[0]
    summed = lax.psum(local_grad, ("edge", "feat"))
    owned = lax.dynamic_slice_in_dim(summed, lax.axis_index("feat") * share, share, 0)
    rows_here = lax.axis_index("feat") * share + lax.broadcasted_iota(jnp.int32, (8, share), 1)
    wanted = 7 * width + lax.broadcasted_iota(jnp.int32, (8, share), 0)
    select = (rows_here == wanted).astype(jnp.float32)
    vector_piece = jnp.dot(
        select, owned, precision=lax.Precision.HIGHEST, preferred_element_type=jnp.float32
    )
    squares, vector_total = lax.psum((jnp.sum(owned * owned), vector_piece), "feat")
    grad_norm = jnp.sqrt(squares)
    factor = jnp.minimum(1.0, MAX_NORM / (grad_norm + 1e-06))
    clipped = owned * factor
    vector_grads = vector_total * factor
    new_first = BETA_ONE * first_moment + (1.0 - BETA_ONE) * clipped
    new_second = BETA_TWO * second_moment + (1.0 - BETA_TWO) * clipped * clipped
    count_steps = step[0].astype(jnp.float32)
    first_hat = new_first / (1.0 - jnp.power(BETA_ONE, count_steps))
    second_hat = new_second / (1.0 - jnp.power(BETA_TWO, count_steps))
    new_params = params - RATE * (
        first_hat / (jnp.sqrt(second_hat) + ADAM_EPS) + WEIGHT_DECAY * params
    )
    decay_now = jnp.minimum(AVERAGE_DECAY, (1.0 + count_steps) / (10.0 + count_steps))
    new_average = decay_now * averaged + (1.0 - decay_now) * new_params
    return (
        new_latents[None],
        grad_latents[None],
        grad_edges[None],
        new_first,
        new_second,
        new_params,
        new_average,
        grad_norm.reshape(1),
        vector_grads,
    )


def solution(mesh):
    placed = (
        P("feat", "edge", None),
        P("feat", "edge", None),
        P("edge"),
        P("edge"),
        P("edge"),
        P("edge"),
        P("feat", None),
        P("feat", None),
        P("feat", None),
        P("feat", None),
        P(),
        P("feat", "edge", None),
    )
    return jax.shard_map(
        on_device,
        mesh=mesh,
        in_specs=placed,
        out_specs=(
            P("feat", "edge", None),
            P("feat", "edge", None),
            P("feat", "edge", None),
            P("feat", None),
            P("feat", None),
            P("feat", None),
            P("feat", None),
            P(),
            P(),
        ),
        check_vma=False,
    )
```

profile of v0, /device:TPU:0, one launch (start us, length us, event | category | flops | bytes accessed | tf_op | source)
XLA Modules:
  0.0 374.1 jit_solution(12631992785596046417)
XLA Ops:
  7.2 1.2 copy.42
  9.0 2.9 collective-permute-start.1
  12.7 1.0 convert_element_type.71
  13.8 22.2 %all_gather.3 = bf16[1824,256]{1,0:T(8,128)(2,1)S(1)} all-gather(bf16[456,256]{1,0:T(8,128)(2,1)S(1)} %convert_element_type.71), channel_id=1, replica_groups=mesh['edge'=8,'feat'=4] {'feat'}, dimensions={0}, use_global_device_ids=true | all-gather | bytes 1167360 | tf_op jit(solution)/shard_map/all_gather | solution.py:117
  36.0 0.9 copy-done.10
  37.0 0.9 pad_maximum_fusion
  37.9 1.4 copy.43
  39.3 17.0 %gather_fusion = bf16[4096,256]{1,0:T(8,128)(2,1)} fusion(bf16[1536,256]{1,0:T(8,128)(2,1)S(1)} %copy.43, s32[4096]{0:T(1024)S(1)} %fusion.66), kind=kCustom, calls=%fused_computation.clone | custom fusion | bytes 4210688 | tf_op jit(solution)/shard_map/jit(_take)/gather | solution.py:55
  56.4 16.9 %gather_fusion.1 = bf16[4096,256]{1,0:T(8,128)(2,1)} fusion(bf16[1536,256]{1,0:T(8,128)(2,1)S(1)} %copy.43, s32[4096]{0:T(1024)S(1)} %fusion.67), kind=kCustom, calls=%fused_computation.1.clone | custom fusion | bytes 4210688 | tf_op jit(solution)/shard_map/jit(_take)/gather | solution.py:55
  73.3 4.0 %fusion.20 = f32[4096,256]{1,0:T(8,128)S(1)} fusion(bf16[4096,256]{1,0:T(8,128)(2,1)} %gather_fusion, pred[4096]{0:T(1024)(128)(4,1)S(1)} %get-tuple-element.86, bf16[1824,256]{1,0:T(8,128)(2,1)} %copy-done.10), kind=kOutput, calls=%fused_computation.49 | convolution fusion | flops 537919488 | bytes 6426624 | tf_op jit(solution)/shard_map/dot_general | solution.py:39
  77.3 1.7 convolution_add_fusion.3
  79.0 1.7 fusion.3
  80.7 4.0 %multiply_convert_fusion = (bf16[4096,256]{1,0:T(8,128)(2,1)S(1)}, f32[4096,256]{1,0:T(8,128)}) fusion(f32[4096,256]{1,0:T(8,128)S(1)} %fusion.3, bf16[1824,256]{1,0:T(8,128)(2,1)} %copy-done.10, s32[4096]{0:T(1024)S(1)} %copy-done.23), kind=kOutput, calls=%fused_computation.30 | convolution fusion | flops 56721408 | bytes 10514432 | tf_op jit(solution)/shard_map/dot_general | solution.py:39
  84.7 1.8 fusion.82
  87.0 1.5 copy-done.1
  88.5 2.7 multiply_add_fusion
  91.2 5.6 %copy.45 = f32[4096,256]{1,0:T(8,128)} copy(f32[4096,256]{0,1:T(8,128)} %multiply_add_fusion) | data formatting | bytes 8388608 | tf_op jit(solution)/shard_map/add | solution.py:71
  96.8 24.1 %scatter_custom_fusion = f32[1536,256]{1,0:T(8,128)} fusion(s32[4096]{0:T(1024)S(1)} %get-tuple-element.58, f32[4096,256]{1,0:T(8,128)} %copy.45, f32[]{:T(128)} %constant.42.clone.1), kind=kCustom, calls=%fused_computation.57 | custom fusion | flops 1048576 | bytes 1573376 | tf_op jit(solution)/shard_map/scatter-add | solution.py:59
  120.9 2.2 fusion.79
  123.2 2.6 collective-permute-start.3
  126.4 1.2 copy.46
  127.7 1.1 fusion.41
  128.8 8.7 %collective-permute-done.2 = f32[512,256]{1,0:T(8,128)S(1)} collective-permute-done((f32[512,256]{1,0:T(8,128)}, f32[512,256]{1,0:T(8,128)S(1)}, u32[]{:S(2)}, u32[]{:S(2)}) %collective-permute-start.2) | collective-permute-done | bytes 524320 | tf_op jit(solution)/shard_map/ppermute | solution.py:35
  137.5 0.8 copy-done.21
  138.3 1.4 fusion.32
  139.8 1.3 multiply_convert_fusion.2
  141.1 1.2 fusion.83
  142.7 1.1 convert_reduce_fusion.3
  143.8 1.0 fusion.86
  144.8 1.2 convert_reduce_fusion.4
  146.1 1.3 convolution_convert_fusion.1
  147.4 2.6 collective-permute-start.5
  150.0 1.0 fusion.85
  151.0 1.0 convolution_bitcast_fusion
  152.0 4.5 %collective-permute-done.4 = bf16[512,256]{1,0:T(8,128)(2,1)S(1)} collective-permute-done((bf16[512,256]{1,0:T(8,128)(2,1)S(1)}, bf16[512,256]{1,0:T(8,128)(2,1)S(1)}, u32[]{:S(2)}, u32[]{:S(2)}) %collective-permute-start.4) | collective-permute-done | bytes 262176 | tf_op jit(solution)/shard_map/ppermute | solution.py:23
  156.6 16.9 %gather_fusion.2 = bf16[4096,256]{1,0:T(8,128)(2,1)} fusion(bf16[1536,256]{1,0:T(8,128)(2,1)S(1)} %pad_maximum_fusion.1, s32[4096]{0:T(1024)S(1)} %fusion.67), kind=kCustom, calls=%fused_computation.2.clone | custom fusion | bytes 4210688 | tf_op jit(solution)/shard_map/jit(_take)/gather | solution.py:55
  173.5 4.1 %copy.48 = bf16[4096,256]{0,1:T(8,128)(2,1)} copy(bf16[4096,256]{1,0:T(8,128)(2,1)} %gather_fusion.2) | data formatting | bytes 4194304 | tf_op jit(solution)/shard_map/jit(_take)/gather | solution.py:55
  177.6 5.3 %fusion.10 = (f32[256]{0:T(256)S(1)}, f32[4096]{0:T(1024)S(1)}, f32[4096]{0:T(1024)S(1)}, f32[256]{0:T(256)S(1)}) fusion(f32[4096,256]{0,1:T(8,128)} %copy-done.1, f32[4096]{0:T(1024)S(1)} %add_rsqrt_fusion, f32[4096]{0:T(1024)S(1)} %broadcast_multiply_fusion.2, bf16[4096,256]{0,1:T(8,128)(2,1)} %copy.48, pred[4096]{0:T(1024)(128)(4,1)S(1)} %get-tuple-element.57, ...), kind=kLoop, calls=%fused_computation.25 | loop fusion | flops 11525632 | bytes 6364160 | tf_op jit(solution)/shard_map/reduce_sum | solution.py:82
  183.0 2.3 convert_reduce_fusion.1
  185.3 1.5 fusion.84
  186.8 0.8 copy-done.25
  187.6 3.0 convert_reduce_fusion.2
  190.6 2.1 fusion.19
  192.9 2.1 fusion.21
  195.1 1.7 fusion.16
  197.1 3.6 fusion.53
  200.8 3.8 %fusion.56 = f32[4096,256]{1,0:T(8,128)} fusion(bf16[4096,256]{1,0:T(8,128)(2,1)S(1)} %get-tuple-element.83, bf16[1824,256]{1,0:T(8,128)(2,1)} %copy-done.10), kind=kOutput, calls=%fused_computation.106 | convolution fusion | flops 536870912 | bytes 6422528 | tf_op jit(solution)/shard_map/dot_general | solution.py:49
  204.6 10.1 %concatenate.11 = f32[1824,256]{1,0:T(8,128)} concatenate(f32[256,256]{1,0:T(8,128)} %fusion.19, f32[256,256]{1,0:T(8,128)} %fusion.21, f32[256,256]{1,0:T(8,128)} %fusion.16, f32[256,256]{1,0:T(8,128)} %fusion.84, f32[256,256]{1,0:T(8,128)S(1)} %copy-done.20, f32[256,256]{1,0:T(8,128)S(1)} %copy-done.19, f32[256,256]{1,0:T(8,128)S(1)} %copy-done.18, f32[1,256]{1,0:T(1,128)S(1)} %bitcast.104, ...), dimensions={0} | concatenate | bytes 3735552 | tf_op jit(solution)/shard_map/concatenate | solution.py:213
  214.7 24.0 %scatter_custom_fusion.2 = f32[1536,256]{1,0:T(8,128)} fusion(s32[4096]{0:T(1024)S(1)} %get-tuple-element.58, f32[4096,256]{1,0:T(8,128)} %fusion.53, f32[]{:T(128)} %constant.42.clone.1), kind=kCustom, calls=%fused_computation.53 | custom fusion | flops 1048576 | bytes 1573376 | tf_op jit(solution)/shard_map/scatter-add | solution.py:59
  238.8 3.1 copy.50
  241.9 24.0 %scatter_custom_fusion.1 = f32[1536,256]{1,0:T(8,128)} fusion(s32[4096]{0:T(1024)S(1)} %get-tuple-element.87, f32[4096,256]{1,0:T(8,128)} %fusion.56, f32[]{:T(128)} %constant.42.clone.1), kind=kCustom, calls=%fused_computation.55 | custom fusion | flops 1048576 | bytes 1573376 | tf_op jit(solution)/shard_map/scatter-add | solution.py:59
  265.9 3.1 copy.49
  269.0 3.4 fusion.78
  272.4 0.8 fusion.80
  273.2 2.6 collective-permute-start.7
  277.1 1.0 copy.51
  278.1 3.7 fusion.5
  282.0 1.4 fusion.30
  283.5 61.5 %all-reduce.3.cloned.1.call-done = f32[1824,256]{1,0:T(8,128)} async-done(((f32[1824,256]{1,0:T(8,128)}), f32[1824,256]{1,0:T(8,128)}) %all-reduce.3.cloned.1.call-update) | async-done | bytes 1867792 | tf_op jit(solution)/shard_map/psum | solution.py:217
  344.9 1.7 multiply_reduce_fusion.4
  346.7 1.9 fusion.38
  348.6 1.0 copy.52
  349.6 12.4 %all-reduce = (f32[]{:T(128)}, f32[8,256]{1,0:T(8,128)S(1)}) all-reduce(f32[]{:T(128)} %multiply_reduce_fusion.4, f32[8,256]{1,0:T(8,128)} %fusion.38), channel_id=1, replica_groups=mesh['edge'=8,'feat'=4] {'feat'}, use_global_device_ids=true, to_apply=%region_21.23 | all-reduce | flops 2049 | bytes 16392 | tf_op jit(solution)/shard_map/psum | solution.py:225
  363.3 2.8 multiply_add_fusion.1
  (82 shorter events, 5.0 us)
Async XLA Ops:
  7.2 71.8 %copy-start = (bf16[1,4096,256]{2,1,0:T(8,128)(2,1)S(1)}, bf16[1,4096,256]{2,1,0:T(8,128)(2,1)}, u32[]{:S(2)}) copy-start(bf16[1,4096,256]{2,1,0:T(8,128)(2,1)} %param.15) | copy-start | bytes 6291460
  7.2 337.8 %all-reduce.3.cloned.1.call-start = ((), (), s32[]{:S(2)}) async-start(), calls=%async_computation | async-start | bytes 3735552 | tf_op jit(solution)/shard_map/psum | solution.py:217
  8.5 28.5 %copy-start.14 = (bf16[1,512,256]{1,2,0:T(8,128)(2,1)}, bf16[1,512,256]{1,2,0:T(8,128)(2,1)S(1)}, u32[]{:S(2)}) copy-start(bf16[1,512,256]{1,2,0:T(8,128)(2,1)S(1)} %copy.42) | copy-start | bytes 786436
  8.5 28.5 %collective-permute-start = (bf16[512,256]{0,1:T(8,128)(2,1)S(1)}, bf16[512,256]{0,1:T(8,128)(2,1)S(1)}, u32[]{:S(2)}, u32[]{:S(2)}) collective-permute-start(bf16[512,256]{0,1:T(8,128)(2,1)S(1)} %bitcast.84), channel_id=1, source_target_pairs={{0,4},{4,8},{8,12},{12,16},{16,20},{20,24},{24,28},{28,0},{1,5},{5... | collective-permute-start | bytes 786440 | tf_op jit(solution)/shard_map/ppermute | solution.py:23
  9.0 28.0 %collective-permute-start.1 = (bf16[512,256]{0,1:T(8,128)(2,1)S(1)}, bf16[512,256]{0,1:T(8,128)(2,1)S(1)}, u32[]{:S(2)}, u32[]{:S(2)}) collective-permute-start(bf16[512,256]{0,1:T(8,128)(2,1)S(1)} %bitcast.85), channel_id=1, source_target_pairs={{4,0},{8,4},{12,8},{16,12},{20,16},{24,20},{28,24},{0,28},{5,1},{9... | collective-permute-start | bytes 786440 | tf_op jit(solution)/shard_map/ppermute | solution.py:25
  36.0 0.9 copy-start.10
  73.3 4.0 %copy-start.8 = (bf16[4096,256]{1,0:T(8,128)(2,1)S(1)}, bf16[4096,256]{1,0:T(8,128)(2,1)}, u32[]{:S(2)}) copy-start(bf16[4096,256]{1,0:T(8,128)(2,1)} %gather_fusion.1) | copy-start | bytes 6291460
  79.0 1.7 copy-start.23
  84.7 1.8 copy-start.6
  86.5 2.0 copy-start.1
  96.8 30.8 %copy-start.24 = (s32[512]{0:T(512)S(1)}, s32[512]{0:T(512)}, u32[]{:S(2)}) copy-start(s32[512]{0:T(512)} %param.19) | copy-start | bytes 6148
  96.8 30.8 %copy-start.13 = (bf16[1,512,256]{2,1,0:T(8,128)(2,1)S(1)}, bf16[1,512,256]{2,1,0:T(8,128)(2,1)}, u32[]{:S(2)}) copy-start(bf16[1,512,256]{2,1,0:T(8,128)(2,1)} %param.14) | copy-start | bytes 786436
  123.2 14.4 %collective-permute-start.2 = (f32[512,256]{1,0:T(8,128)}, f32[512,256]{1,0:T(8,128)S(1)}, u32[]{:S(2)}, u32[]{:S(2)}) collective-permute-start(f32[512,256]{1,0:T(8,128)} %get-tuple-element.61), channel_id=1, source_target_pairs={{0,4},{4,8},{8,12},{12,16},{16,20},{20,24},{24,28},{28,0},{1,5},{5... | collective-permute-start | bytes 1572872 | tf_op jit(solution)/shard_map/ppermute | solution.py:35
  123.2 15.2 %collective-permute-start.3 = (f32[512,256]{1,0:T(8,128)}, f32[512,256]{1,0:T(8,128)}, u32[]{:S(2)}, u32[]{:S(2)}) collective-permute-start(f32[512,256]{1,0:T(8,128)} %get-tuple-element.62), channel_id=1, source_target_pairs={{0,28},{4,0},{8,4},{12,8},{16,12},{20,16},{24,20},{28,24},{1,29},{... | collective-permute-start | bytes 1572872 | tf_op jit(solution)/shard_map/ppermute | solution.py:35
  137.5 0.8 copy-start.21
  139.8 2.9 copy-start.15
  146.0 10.5 %copy-start.11 = (bf16[512,256]{1,0:T(8,128)(2,1)}, bf16[512,256]{1,0:T(8,128)(2,1)S(1)}, u32[]{:S(2)}) copy-start(bf16[512,256]{1,0:T(8,128)(2,1)S(1)} %get-tuple-element.85) | copy-start | bytes 786436
  147.3 9.2 %collective-permute-start.4 = (bf16[512,256]{1,0:T(8,128)(2,1)S(1)}, bf16[512,256]{1,0:T(8,128)(2,1)S(1)}, u32[]{:S(2)}, u32[]{:S(2)}) collective-permute-start(bf16[512,256]{1,0:T(8,128)(2,1)S(1)} %convolution_convert_fusion.1), channel_id=1, source_target_pairs={{0,4},{4,8},{8,12},{12,16},{16,20},{20,24},{24,28},{28,0},{1,5},{5... | collective-permute-start | bytes 786440 | tf_op jit(solution)/shard_map/ppermute | solution.py:23
  147.4 9.1 %collective-permute-start.5 = (bf16[512,256]{1,0:T(8,128)(2,1)S(1)}, bf16[512,256]{1,0:T(8,128)(2,1)S(1)}, u32[]{:S(2)}, u32[]{:S(2)}) collective-permute-start(bf16[512,256]{1,0:T(8,128)(2,1)S(1)} %convolution_convert_fusion.1), channel_id=1, source_target_pairs={{4,0},{8,4},{12,8},{16,12},{20,16},{24,20},{28,24},{0,28},{5,1},{9... | collective-permute-start | bytes 786440 | tf_op jit(solution)/shard_map/ppermute | solution.py:25
  177.6 5.4 %copy-start.2 = (f32[4096,256]{0,1:T(8,128)S(1)}, f32[4096,256]{0,1:T(8,128)}, u32[]{:S(2)}) copy-start(f32[4096,256]{0,1:T(8,128)} %copy-done.1) | copy-start | bytes 12582916
  177.6 5.4 %copy-start.4 = (bf16[4096,256]{0,1:T(8,128)(2,1)S(1)}, bf16[4096,256]{0,1:T(8,128)(2,1)}, u32[]{:S(2)}) copy-start(bf16[4096,256]{0,1:T(8,128)(2,1)} %copy.48) | copy-start | bytes 6291460
  183.0 2.3 copy-start.7
  185.3 2.3 copy-start.25
  187.6 3.0 copy-start.5
  190.6 10.2 %copy-start.3 = (bf16[4096,256]{1,0:T(8,128)(2,1)}, bf16[4096,256]{1,0:T(8,128)(2,1)S(1)}, u32[]{:S(2)}) copy-start(bf16[4096,256]{1,0:T(8,128)(2,1)S(1)} %get-tuple-element.83) | copy-start | bytes 6291460
  190.6 2.3 copy-start.9
  200.8 3.8 %copy-start.18 = (f32[256,256]{1,0:T(8,128)S(1)}, f32[256,256]{1,0:T(8,128)}, u32[]{:S(2)}) copy-start(f32[256,256]{1,0:T(8,128)} %fusion.86) | copy-start | bytes 786436
  200.8 3.8 %copy-start.19 = (f32[256,256]{1,0:T(8,128)S(1)}, f32[256,256]{1,0:T(8,128)}, u32[]{:S(2)}) copy-start(f32[256,256]{1,0:T(8,128)} %fusion.85) | copy-start | bytes 786436
  200.8 3.8 %copy-start.20 = (f32[256,256]{1,0:T(8,128)S(1)}, f32[256,256]{1,0:T(8,128)}, u32[]{:S(2)}) copy-start(f32[256,256]{1,0:T(8,128)} %convolution_bitcast_fusion) | copy-start | bytes 786436
  269.0 8.2 %copy-start.16 = (f32[1,512,256]{1,2,0:T(8,128)S(1)}, f32[1,512,256]{1,2,0:T(8,128)}, u32[]{:S(2)}) copy-start(f32[1,512,256]{1,2,0:T(8,128)} %get-tuple-element.65) | copy-start | bytes 1572868
  273.2 8.8 %collective-permute-start.6 = (bf16[512,256]{0,1:T(8,128)(2,1)}, bf16[512,256]{0,1:T(8,128)(2,1)S(1)}, u32[]{:S(2)}, u32[]{:S(2)}) collective-permute-start(bf16[512,256]{0,1:T(8,128)(2,1)} %get-tuple-element.63), channel_id=1, source_target_pairs={{0,4},{4,8},{8,12},{12,16},{16,20},{20,24},{24,28},{28,0},{1,5},{5... | collective-permute-start | bytes 786440 | tf_op jit(solution)/shard_map/ppermute | solution.py:35
  273.2 8.8 %collective-permute-start.7 = (bf16[512,256]{0,1:T(8,128)(2,1)}, bf16[512,256]{0,1:T(8,128)(2,1)}, u32[]{:S(2)}, u32[]{:S(2)}) collective-permute-start(bf16[512,256]{0,1:T(8,128)(2,1)} %get-tuple-element.64), channel_id=1, source_target_pairs={{0,28},{4,0},{8,4},{12,8},{16,12},{20,16},{24,20},{28,24},{1,29},{... | collective-permute-start | bytes 786440 | tf_op jit(solution)/shard_map/ppermute | solution.py:35
  278.1 3.9 %copy-start.12 = (bf16[512,256]{1,0:T(8,128)(2,1)S(1)}, bf16[512,256]{1,0:T(8,128)(2,1)}, u32[]{:S(2)}) copy-start(bf16[512,256]{1,0:T(8,128)(2,1)} %copy-done.11) | copy-start | bytes 786436
  283.5 79.8 %copy-start.17 = (f32[456,256]{1,0:T(8,128)S(1)}, f32[456,256]{1,0:T(8,128)}, u32[]{:S(2)}) copy-start(f32[456,256]{1,0:T(8,128)} %param.20) | copy-start | bytes 1400836
  283.5 79.8 %copy-start.22 = (f32[456,256]{1,0:T(8,128)S(1)}, f32[456,256]{1,0:T(8,128)}, u32[]{:S(2)}) copy-start(f32[456,256]{1,0:T(8,128)} %param.23) | copy-start | bytes 1400836
Sparse Core Ops, SparseCore 0:
  214.8 130.0 all-reduce.2
where the time goes:
time: 375 us; the launch traced here: 374 us
  other arithmetic  98.5 us (26%)
  local copies, waits for them, and re-layouts  90 us (24%)
  waiting for transfers between devices  74.9 us (20%)
  matrix products  47.4 us (13%)
  blocking collectives  34.6 us (9%)
  between operations  17.2 us (5%)
  starting transfers between devices  11.5 us (3%)
    scatter-add x3, other arithmetic, add_rows(): return jax.ops.segment_sum(values, indices, num_segments=rows)  72.2 us
    psum x1, waiting for transfers between devices, on_device(): summed = lax.psum(local_grad, ('edge', 'feat'))  61.5 us
    gather x4, local copies, waits for them, and re-layouts, pick_rows(): return jnp.take(table, indices, axis=0)  55 us
    all_gather x1, blocking collectives, on_device(): lax.all_gather(params.astype(jnp.bfloat16), 'feat', axis=0, tiled=True)  22.2 us
    dot_general x7, matrix products, product_transposed(): lax.dot_general(left, right, (((1,), (1,)), ((), ())), preferred_element_...  18 us
    dot_general x8, matrix products, product(): return jnp.dot(left, right, preferred_element_type=jnp.float32)  16.7 us
    psum x1, blocking collectives, on_device(): lax.psum((jnp.sum(owned * owned), vector_piece), 'feat')  12.4 us
    dot_general x8, matrix products, outer_product(): lax.dot_general(left, right, (((0,), (0,)), ((), ())), preferred_element_...  10.7 us
  transfers between devices with their start and end apart: 9, of which 4 were waited for; matrix products, arithmetic and copies ran while one was open for 19% of the time, Pallas kernels for 0%

commit v1 on v0

--- a/solution.py
+++ b/solution.py
@@ -214,7 +214,8 @@
         [g_first, g_second, g_node_first, g_node_second, vector_rows, g_table], axis=0
     )
     share = params.shape[0]
-    summed = lax.psum(local_grad, ("edge", "feat"))
+    parts = lax.all_gather(local_grad, ("edge", "feat"), axis=0, tiled=False)
+    summed = parts.sum(axis=0)
     owned = lax.dynamic_slice_in_dim(summed, lax.axis_index("feat") * share, share, 0)
     rows_here = lax.axis_index("feat") * share + lax.broadcasted_iota(jnp.int32, (8, share), 1)
     wanted = 7 * width + lax.broadcasted_iota(jnp.int32, (8, share), 0)

time: 375 us -> 586 us (1.56); the launches traced: 374 us -> 577 us
  waiting for transfers between devices: 74.9 us -> 262 us
  other arithmetic: 98.5 us -> 118 us
    all_gather x0 -> x1, waiting for transfers between devices: none -> 241 us  [on_device(): parts = lax.all_gather(local_grad, ('edge', 'feat'), axis=0, tiled=False)]
    psum x1 -> x0, waiting for transfers between devices: 61.5 us -> none  [on_device(): summed = lax.psum(local_grad, ('edge', 'feat'))]
    reduce_sum x0 -> x1, other arithmetic: none -> 20.2 us  [on_device(): summed = parts.sum(axis=0)]
    ppermute x4, waiting for transfers between devices: 8.93 us -> 17.3 us  [passed_along(): return lax.ppermute(value, axis, pairs)]
  transfers between devices with their start and end apart: 9 -> 9, of which waited for: 4 -> 7; matrix products, arithmetic and copies ran while one was open for 19% -> 14% of each run, Pallas kernels for 0% -> 0%
where the time goes in v1:
time: 586 us; the launch traced here: 577 us
  waiting for transfers between devices  262 us (45%)
  other arithmetic  118 us (20%)
  local copies, waits for them, and re-layouts  90.1 us (15%)
  matrix products  48.7 us (8%)
  blocking collectives  32.2 us (5%)
  between operations  17.3 us (3%)
  starting transfers between devices  8.29 us (1%)
    all_gather x1, waiting for transfers between devices, on_device(): parts = lax.all_gather(local_grad, ('edge', 'feat'), axis=0, tiled=False)  241 us
    scatter-add x3, other arithmetic, add_rows(): return jax.ops.segment_sum(values, indices, num_segments=rows)  72.3 us
    gather x4, local copies, waits for them, and re-layouts, pick_rows(): return jnp.take(table, indices, axis=0)  55 us
    all_gather x1, blocking collectives, on_device(): lax.all_gather(params.astype(jnp.bfloat16), 'feat', axis=0, tiled=True)  21.5 us
    reduce_sum x1, other arithmetic, on_device(): summed = parts.sum(axis=0)  20.2 us
    dot_general x7, matrix products, product_transposed(): lax.dot_general(left, right, (((1,), (1,)), ((), ())), preferred_element_...  19.3 us
    ppermute x4, waiting for transfers between devices, passed_along(): return lax.ppermute(value, axis, pairs)  17.3 us
    dot_general x8, matrix products, product(): return jnp.dot(left, right, preferred_element_type=jnp.float32)  16.7 us
  transfers between devices with their start and end apart: 9, of which 7 were waited for; matrix products, arithmetic and copies ran while one was open for 14% of the time, Pallas kernels for 0%

profile of v1, /device:TPU:0, one launch (start us, length us, event | category | flops | bytes accessed | tf_op | source)
XLA Modules:
  0.0 577.3 jit_solution(6067547649934212919)
XLA Ops:
  7.3 1.2 copy.42
  8.5 3.4 collective-permute-start.1
  11.9 1.0 convert_element_type.71
  12.9 21.5 %all_gather.9 = bf16[1824,256]{1,0:T(8,128)(2,1)S(1)} all-gather(bf16[456,256]{1,0:T(8,128)(2,1)S(1)} %convert_element_type.71), channel_id=1, replica_groups=mesh['edge'=8,'feat'=4] {'feat'}, dimensions={0}, use_global_device_ids=true | all-gather | bytes 1167360 | tf_op jit(solution)/shard_map/all_gather | solution.py:117
  34.4 1.0 copy-done.10
  35.5 0.9 pad_maximum_fusion
  36.5 1.4 copy.43
  37.9 17.0 %gather_fusion = bf16[4096,256]{1,0:T(8,128)(2,1)} fusion(bf16[1536,256]{1,0:T(8,128)(2,1)S(1)} %copy.43, s32[4096]{0:T(1024)S(1)} %fusion.66), kind=kCustom, calls=%fused_computation.clone | custom fusion | bytes 4210688 | tf_op jit(solution)/shard_map/jit(_take)/gather | solution.py:55
  54.9 16.9 %gather_fusion.1 = bf16[4096,256]{1,0:T(8,128)(2,1)} fusion(bf16[1536,256]{1,0:T(8,128)(2,1)S(1)} %copy.43, s32[4096]{0:T(1024)S(1)} %fusion.67), kind=kCustom, calls=%fused_computation.1.clone | custom fusion | bytes 4210688 | tf_op jit(solution)/shard_map/jit(_take)/gather | solution.py:55
  71.8 4.0 fusion.20
  75.9 1.7 convolution_add_fusion.3
  77.6 1.7 fusion.3
  79.3 4.0 multiply_convert_fusion
  83.2 1.8 fusion.82
  85.6 1.5 copy-done.1
  87.1 2.7 multiply_add_fusion
  89.8 5.6 copy.45
  95.4 24.1 %scatter_custom_fusion = f32[1536,256]{1,0:T(8,128)} fusion(s32[4096]{0:T(1024)S(1)} %get-tuple-element.58, f32[4096,256]{1,0:T(8,128)} %copy.45, f32[]{:T(128)} %constant.42.clone.1), kind=kCustom, calls=%fused_computation.57 | custom fusion | flops 1048576 | bytes 1573376 | tf_op jit(solution)/shard_map/scatter-add | solution.py:59
  119.5 2.2 fusion.79
  123.0 1.2 copy.46
  124.3 1.1 fusion.41
  125.4 9.2 %collective-permute-done.3 = f32[512,256]{1,0:T(8,128)S(1)} collective-permute-done((f32[512,256]{1,0:T(8,128)}, f32[512,256]{1,0:T(8,128)S(1)}, u32[]{:S(2)}, u32[]{:S(2)}) %collective-permute-start.3) | collective-permute-done | bytes 524320 | tf_op jit(solution)/shard_map/ppermute | solution.py:35
  135.5 1.4 fusion.32
  137.0 1.3 multiply_convert_fusion.2
  138.2 1.2 fusion.83
  139.9 1.1 convert_reduce_fusion.3
  141.0 1.2 convert_reduce_fusion.4
  142.3 1.3 convolution_convert_fusion.1
  143.5 2.6 collective-permute-start.5
  146.1 1.0 convolution_bitcast_fusion
  147.1 1.0 fusion.85
  148.0 1.0 fusion.86
  149.0 1.6 collective-permute-done.5
  150.7 2.1 collective-permute-done.4
  152.8 16.9 %gather_fusion.2 = bf16[4096,256]{1,0:T(8,128)(2,1)} fusion(bf16[1536,256]{1,0:T(8,128)(2,1)S(1)} %pad_maximum_fusion.1, s32[4096]{0:T(1024)S(1)} %fusion.67), kind=kCustom, calls=%fused_computation.2.clone | custom fusion | bytes 4210688 | tf_op jit(solution)/shard_map/jit(_take)/gather | solution.py:55
  169.8 4.1 copy.48
  173.9 5.3 fusion.10
  179.3 2.3 convert_reduce_fusion.1
  181.6 3.0 convert_reduce_fusion.2
  184.6 2.1 fusion.19
  186.9 2.2 fusion.21
  189.1 1.7 fusion.16
  190.7 1.5 fusion.84
  193.3 10.1 %concatenate.11 = f32[1824,256]{1,0:T(8,128)} concatenate(f32[256,256]{1,0:T(8,128)} %fusion.19, f32[256,256]{1,0:T(8,128)} %fusion.21, f32[256,256]{1,0:T(8,128)} %fusion.16, f32[256,256]{1,0:T(8,128)} %fusion.84, f32[256,256]{1,0:T(8,128)S(1)} %copy-done.18, f32[256,256]{1,0:T(8,128)S(1)} %copy-done.19, f32[256,256]{1,0:T(8,128)S(1)} %copy-done.20, f32[1,256]{1,0:T(1,128)S(1)} %bitcast.106, ...), dimensions={0} | concatenate | bytes 3735552 | tf_op jit(solution)/shard_map/concatenate | solution.py:213
  204.0 4.4 fusion.56
  208.4 24.2 %scatter_custom_fusion.1 = f32[1536,256]{1,0:T(8,128)} fusion(s32[4096]{0:T(1024)S(1)} %get-tuple-element.87, f32[4096,256]{1,0:T(8,128)} %fusion.56, f32[]{:T(128)} %constant.42.clone.1), kind=kCustom, calls=%fused_computation.55 | custom fusion | flops 1048576 | bytes 1573376 | tf_op jit(solution)/shard_map/scatter-add | solution.py:59
  232.6 3.1 copy.49
  235.7 4.4 fusion.53
  240.1 24.0 %scatter_custom_fusion.2 = f32[1536,256]{1,0:T(8,128)} fusion(s32[4096]{0:T(1024)S(1)} %get-tuple-element.58, f32[4096,256]{1,0:T(8,128)} %fusion.53, f32[]{:T(128)} %constant.42.clone.1), kind=kCustom, calls=%fused_computation.53 | custom fusion | flops 1048576 | bytes 1573376 | tf_op jit(solution)/shard_map/scatter-add | solution.py:59
  264.1 3.2 copy.50
  267.3 3.4 fusion.78
  271.5 1.0 collective-permute-start.7
  273.9 1.0 copy.51
  274.9 3.7 fusion.5
  278.6 6.1 %collective-permute-done.7 = bf16[512,256]{0,1:T(8,128)(2,1)S(1)} collective-permute-done((bf16[512,256]{0,1:T(8,128)(2,1)}, bf16[512,256]{0,1:T(8,128)(2,1)S(1)}, u32[]{:S(2)}, u32[]{:S(2)}) %collective-permute-start.7) | collective-permute-done | bytes 262176 | tf_op jit(solution)/shard_map/ppermute | solution.py:35
  284.7 1.8 collective-permute-done.6
  286.6 1.4 fusion.30
  288.0 241.3 %all-gather.3.cloned.1.call-done = f32[58368,256]{1,0:T(8,128)} async-done(((f32[1824,256]{1,0:T(8,128)}), f32[58368,256]{1,0:T(8,128)}) %all-gather.3.cloned.1.call-update) | async-done | bytes 59768848 | tf_op jit(solution)/shard_map/all_gather | solution.py:217
  529.4 20.2 %reduce_sum.194 = f32[1824,256]{1,0:T(8,128)} reduce(f32[32,1824,256]{2,1,0:T(8,128)} %bitcast.85, f32[]{:T(128)} %constant.42.clone.1), dimensions={0}, to_apply=%region_19.21 | reduce | flops 14475264 | bytes 61636612 | tf_op jit(solution)/shard_map/reduce_sum | solution.py:218
  549.6 1.8 multiply_reduce_fusion.4
  551.4 1.9 fusion.38
  553.3 1.0 copy.52
  554.3 10.7 %all-reduce = (f32[]{:T(128)}, f32[8,256]{1,0:T(8,128)S(1)}) all-reduce(f32[]{:T(128)} %multiply_reduce_fusion.4, f32[8,256]{1,0:T(8,128)} %fusion.38), channel_id=1, replica_groups=mesh['edge'=8,'feat'=4] {'feat'}, use_global_device_ids=true, to_apply=%region_21.23 | all-reduce | flops 2049 | bytes 16392 | tf_op jit(solution)/shard_map/psum | solution.py:226
  566.3 2.8 multiply_add_fusion.1
  (87 shorter events, 7.3 us)
Async XLA Ops:
  7.2 70.4 %copy-start = (bf16[1,4096,256]{2,1,0:T(8,128)(2,1)S(1)}, bf16[1,4096,256]{2,1,0:T(8,128)(2,1)}, u32[]{:S(2)}) copy-start(bf16[1,4096,256]{2,1,0:T(8,128)(2,1)} %param.15) | copy-start | bytes 6291460
  7.2 28.2 %copy-start.24 = (s32[4096]{0:T(1024)S(1)}, s32[4096]{0:T(1024)}, u32[]{:S(2)}) copy-start(s32[4096]{0:T(1024)} %param.17) | copy-start | bytes 49156
  7.2 28.2 %copy-start.25 = (s32[4096]{0:T(1024)S(1)}, s32[4096]{0:T(1024)}, u32[]{:S(2)}) copy-start(s32[4096]{0:T(1024)} %param.16) | copy-start | bytes 49156
  7.2 522.2 %all-gather.3.cloned.1.call-start = ((), (), s32[]{:S(2)}) async-start(), calls=%async_computation | async-start | bytes 61636608 | tf_op jit(solution)/shard_map/all_gather | solution.py:217
  8.5 27.0 %copy-start.14 = (bf16[1,512,256]{1,2,0:T(8,128)(2,1)}, bf16[1,512,256]{1,2,0:T(8,128)(2,1)S(1)}, u32[]{:S(2)}) copy-start(bf16[1,512,256]{1,2,0:T(8,128)(2,1)S(1)} %copy.42) | copy-start | bytes 786436
  8.5 27.0 %collective-permute-start.1 = (bf16[512,256]{0,1:T(8,128)(2,1)S(1)}, bf16[512,256]{0,1:T(8,128)(2,1)S(1)}, u32[]{:S(2)}, u32[]{:S(2)}) collective-permute-start(bf16[512,256]{0,1:T(8,128)(2,1)S(1)} %bitcast.86), channel_id=1, source_target_pairs={{4,0},{8,4},{12,8},{16,12},{20,16},{24,20},{28,24},{0,28},{5,1},{9... | collective-permute-start | bytes 786440 | tf_op jit(solution)/shard_map/ppermute | solution.py:25
  11.9 23.6 %collective-permute-start = (bf16[512,256]{0,1:T(8,128)(2,1)S(1)}, bf16[512,256]{0,1:T(8,128)(2,1)S(1)}, u32[]{:S(2)}, u32[]{:S(2)}) collective-permute-start(bf16[512,256]{0,1:T(8,128)(2,1)S(1)} %bitcast.87), channel_id=1, source_target_pairs={{0,4},{4,8},{8,12},{12,16},{16,20},{20,24},{24,28},{28,0},{1,5},{5... | collective-permute-start | bytes 786440 | tf_op jit(solution)/shard_map/ppermute | solution.py:23
  34.4 1.0 copy-start.10
  71.8 4.0 copy-start.8
  77.6 1.7 copy-start.23
  83.2 1.8 copy-start.6
  85.1 2.0 copy-start.1
  95.4 28.8 %copy-start.26 = (s32[512]{0:T(512)S(1)}, s32[512]{0:T(512)}, u32[]{:S(2)}) copy-start(s32[512]{0:T(512)} %param.19) | copy-start | bytes 6148
  95.4 28.9 %copy-start.13 = (bf16[1,512,256]{2,1,0:T(8,128)(2,1)S(1)}, bf16[1,512,256]{2,1,0:T(8,128)(2,1)}, u32[]{:S(2)}) copy-start(bf16[1,512,256]{2,1,0:T(8,128)(2,1)} %param.14) | copy-start | bytes 786436
  121.7 12.8 %collective-permute-start.3 = (f32[512,256]{1,0:T(8,128)}, f32[512,256]{1,0:T(8,128)S(1)}, u32[]{:S(2)}, u32[]{:S(2)}) collective-permute-start(f32[512,256]{1,0:T(8,128)} %get-tuple-element.62), channel_id=1, source_target_pairs={{0,28},{4,0},{8,4},{12,8},{16,12},{20,16},{24,20},{28,24},{1,29},{... | collective-permute-start | bytes 1572872 | tf_op jit(solution)/shard_map/ppermute | solution.py:35
  122.6 12.9 %collective-permute-start.2 = (f32[512,256]{1,0:T(8,128)}, f32[512,256]{1,0:T(8,128)}, u32[]{:S(2)}, u32[]{:S(2)}) collective-permute-start(f32[512,256]{1,0:T(8,128)} %get-tuple-element.61), channel_id=1, source_target_pairs={{0,4},{4,8},{8,12},{12,16},{16,20},{20,24},{24,28},{28,0},{1,5},{5... | collective-permute-start | bytes 1572872 | tf_op jit(solution)/shard_map/ppermute | solution.py:35
  134.6 0.8 copy-start.21
  137.0 2.9 copy-start.15
  142.2 8.4 %copy-start.11 = (bf16[512,256]{1,0:T(8,128)(2,1)}, bf16[512,256]{1,0:T(8,128)(2,1)S(1)}, u32[]{:S(2)}) copy-start(bf16[512,256]{1,0:T(8,128)(2,1)S(1)} %get-tuple-element.85) | copy-start | bytes 786436
  143.5 7.1 %collective-permute-start.5 = (bf16[512,256]{1,0:T(8,128)(2,1)S(1)}, bf16[512,256]{1,0:T(8,128)(2,1)S(1)}, u32[]{:S(2)}, u32[]{:S(2)}) collective-permute-start(bf16[512,256]{1,0:T(8,128)(2,1)S(1)} %convolution_convert_fusion.1), channel_id=1, source_target_pairs={{4,0},{8,4},{12,8},{16,12},{20,16},{24,20},{28,24},{0,28},{5,1},{9... | collective-permute-start | bytes 786440 | tf_op jit(solution)/shard_map/ppermute | solution.py:25
  146.1 6.7 %collective-permute-start.4 = (bf16[512,256]{1,0:T(8,128)(2,1)S(1)}, bf16[512,256]{1,0:T(8,128)(2,1)S(1)}, u32[]{:S(2)}, u32[]{:S(2)}) collective-permute-start(bf16[512,256]{1,0:T(8,128)(2,1)S(1)} %convolution_convert_fusion.1), channel_id=1, source_target_pairs={{0,4},{4,8},{8,12},{12,16},{16,20},{20,24},{24,28},{28,0},{1,5},{5... | collective-permute-start | bytes 786440 | tf_op jit(solution)/shard_map/ppermute | solution.py:23
  173.9 5.4 copy-start.2
  173.9 5.4 copy-start.4
  179.3 2.3 copy-start.27
  181.6 3.0 copy-start.5
  184.6 7.7 %copy-start.3 = (bf16[4096,256]{1,0:T(8,128)(2,1)}, bf16[4096,256]{1,0:T(8,128)(2,1)S(1)}, u32[]{:S(2)}) copy-start(bf16[4096,256]{1,0:T(8,128)(2,1)S(1)} %get-tuple-element.83) | copy-start | bytes 6291460
  184.6 2.3 copy-start.9
  189.1 1.7 copy-start.7
  192.2 1.0 copy-start.18
  192.2 1.0 copy-start.19
  192.2 1.1 copy-start.20
  267.3 6.6 %copy-start.16 = (f32[1,512,256]{1,2,0:T(8,128)S(1)}, f32[1,512,256]{1,2,0:T(8,128)}, u32[]{:S(2)}) copy-start(f32[1,512,256]{1,2,0:T(8,128)} %get-tuple-element.65) | copy-start | bytes 1572868
  271.5 13.2 %collective-permute-start.7 = (bf16[512,256]{0,1:T(8,128)(2,1)}, bf16[512,256]{0,1:T(8,128)(2,1)S(1)}, u32[]{:S(2)}, u32[]{:S(2)}) collective-permute-start(bf16[512,256]{0,1:T(8,128)(2,1)} %get-tuple-element.64), channel_id=1, source_target_pairs={{0,28},{4,0},{8,4},{12,8},{16,12},{20,16},{24,20},{28,24},{1,29},{... | collective-permute-start | bytes 786440 | tf_op jit(solution)/shard_map/ppermute | solution.py:35
  272.6 14.0 %collective-permute-start.6 = (bf16[512,256]{0,1:T(8,128)(2,1)}, bf16[512,256]{0,1:T(8,128)(2,1)}, u32[]{:S(2)}, u32[]{:S(2)}) collective-permute-start(bf16[512,256]{0,1:T(8,128)(2,1)} %get-tuple-element.63), channel_id=1, source_target_pairs={{0,4},{4,8},{8,12},{12,16},{16,20},{20,24},{24,28},{28,0},{1,5},{5... | collective-permute-start | bytes 786440 | tf_op jit(solution)/shard_map/ppermute | solution.py:35
  274.9 11.7 %copy-start.12 = (bf16[512,256]{1,0:T(8,128)(2,1)S(1)}, bf16[512,256]{1,0:T(8,128)(2,1)}, u32[]{:S(2)}) copy-start(bf16[512,256]{1,0:T(8,128)(2,1)} %copy-done.11) | copy-start | bytes 786436
  549.6 16.8 %copy-start.17 = (f32[456,256]{1,0:T(8,128)S(1)}, f32[456,256]{1,0:T(8,128)}, u32[]{:S(2)}) copy-start(f32[456,256]{1,0:T(8,128)} %param.20) | copy-start | bytes 1400836
  549.6 16.8 %copy-start.22 = (f32[456,256]{1,0:T(8,128)S(1)}, f32[456,256]{1,0:T(8,128)}, u32[]{:S(2)}) copy-start(f32[456,256]{1,0:T(8,128)} %param.23) | copy-start | bytes 1400836
Sparse Core Ops, SparseCore 0:
  203.5 325.8 all-gather.2
